TPU v7x, 32 devices: a whole 2x2x4 slice. The times are simulated.
32 devices in a mesh: group: 2 (over y), chan: 8 (over z, x), rec: 2 (over core).
Axes of the slice: x: 2, y: 2, z: 4, core: 2. Of those that a mesh axis runs over, the one named last changes fastest.
Arguments:
- records: bfloat16 [256, 128, 1024], P(('group', 'chan'), 'rec'), parts along dimension 0, may hold values from -50 to 50
- valid: int32 [256, 128], P(('group', 'chan'), 'rec'), parts along dimension 0, may hold values 0 or 1
- sources: int32 [16], P('group'), parts along dimension 0, may hold values from 0 to 127, as said below
Outputs:
- cross: float32 [256, 8, 1024], P(('group', 'chan'), None, 'rec'), parts along dimension 0
There are 2 independent parts, one for each index of `group`. A program takes and returns all parts, laid end to end along the dimension named above; each array names one. Nothing has to cross between parts.
Inputs may be any that keep to these rules, and one draw needn't show every extreme that they name: `sources`: 8 distinct channel numbers.
All inputs are finite; a program needn't handle non-finite values. No bound on the sum of `valid` on one device may be relied on, other than what follows from the above.
Results may differ from a plain program's by a relative error of at most 0.0034.
Values may be sent and summed in bfloat16 or wider, within the bound.
No kernel may reach another device: no remote copies, remote signals or barrier semaphores. Data moves between devices by JAX's collectives and lax.ppermute only.
A program may use at most 64 MiB of HBM per device.

v0:
```python
import math
import jax
import jax.numpy as jnp
from jax import lax
from jax.sharding import PartitionSpec as P


def dft_table(length, bins):
    times = jnp.arange(length, dtype=jnp.int32)[:, None]
    freqs = jnp.arange(bins, dtype=jnp.int32)[None, :]
    phase = (times * freqs % length).astype(jnp.float32) * (2.0 * math.pi / length)
    return jnp.concatenate([jnp.cos(phase), -jnp.sin(phase)], axis=1).astype(jnp.bfloat16)


def transform(rows, table):
    lead = rows.shape[:-1]
    flat = rows.reshape(-1, rows.shape[-1])
    return jnp.dot(flat, table, preferred_element_type=jnp.float32).reshape(
        lead + (table.shape[1],)
    )


def whiten(spec, bins):
    real_part = spec[..., :bins]
    imag_part = spec[..., bins:]
    power = jnp.mean(real_part * real_part + imag_part * imag_part, axis=-1, keepdims=True)
    return (spec * lax.rsqrt(power + 1e-06)).astype(jnp.bfloat16)


def spread(picked):
    return lax.psum(picked.astype(jnp.float32), "chan").astype(jnp.bfloat16)


def per_device(records, valid, sources):
    per_dev, rec_rows, length = records.shape
    bins = length // 2
    table = dft_table(length, bins)
    masked = records * valid[:, :, None].astype(jnp.bfloat16)
    first = lax.axis_index("chan") * per_dev
    owned = sources[:, None] == first + jnp.arange(per_dev, dtype=jnp.int32)[None, :]
    picked = jnp.einsum(
        "sc,crl->srl", owned.astype(jnp.bfloat16), masked, preferred_element_type=jnp.float32
    ).astype(jnp.bfloat16)
    arrived = spread(picked)
    spectra = transform(masked, table)
    wsrc = whiten(transform(arrived, table), bins)
    hp = lax.Precision.HIGHEST
    xr = spectra[..., :bins]
    xi = spectra[..., bins:]
    wr = wsrc[..., :bins].astype(jnp.float32)
    wi = wsrc[..., bins:].astype(jnp.float32)
    real_sum = jnp.einsum("crf,srf->csf", xr, wr, precision=hp) + jnp.einsum(
        "crf,srf->csf", xi, wi, precision=hp
    )
    imag_sum = jnp.einsum("crf,srf->csf", xi, wr, precision=hp) - jnp.einsum(
        "crf,srf->csf", xr, wi, precision=hp
    )
    partial_stack = jnp.concatenate([real_sum, imag_sum], axis=-1)
    total = lax.psum_scatter(partial_stack, "rec", scatter_dimension=2, tiled=True)
    return total / (rec_rows * lax.axis_size("rec"))


def solution(mesh):
    placed = (P(("group", "chan"), "rec", None), P(("group", "chan"), "rec"), P("group"))
    return jax.shard_map(
        per_device,
        mesh=mesh,
        in_specs=placed,
        out_specs=P(("group", "chan"), None, "rec"),
        check_vma=False,
    )
```

profile of v0, /device:TPU:0, one launch (start us, length us, event | category | flops | bytes accessed | tf_op | source)
XLA Modules:
  0.0 171.4 jit_solution(13488486058295633462)
XLA Ops:
  6.5 0.0 copy-start.4
  6.5 0.0 reduce-scatter.2.cloned.1.call-start
  6.5 9.3 %negate_convert_fusion = (bf16[1024,512]{1,0:T(8,128)(2,1)}, bf16[1024,512]{1,0:T(8,128)(2,1)}) fusion(), kind=kLoop, calls=%fused_computation.13 | loop fusion | flops 8912896 | bytes 2097152 | tf_op jit(solution)/shard_map/convert.1
  15.8 0.0 copy-done.4
  15.8 0.0 copy-start.5
  15.9 1.8 %broadcast_multiply_fusion = bf16[16,64,1024]{2,1,0:T(8,128)(2,1)S(1)} fusion(bf16[16,64,1024]{2,1,0:T(8,128)(2,1)} %param.3, bf16[16,64]{1,0:T(8,128)(2,1)S(1)} %convert_element_type.25), kind=kLoop, calls=%fused_computation.26 | loop fusion | flops 1048576 | bytes 4196352 | tf_op jit(solution)/shard_map/mul | solution.py:38
  17.7 0.0 copy-done.5
  17.7 1.3 fusion.3
  18.9 2.0 %fusion.10 = f32[8,64,1024]{2,1,0:T(8,128)} fusion(bf16[8,64,1024]{2,0,1:T(8,128)(2,1)S(1)} %fusion.3), kind=kLoop, calls=%fused_computation.20 | loop fusion | flops 524288 | bytes 3145728 | tf_op jit(solution)/shard_map/convert_element_type | solution.py:31
  20.9 94.7 %all-reduce.1 = bf16[8,64,1024]{2,1,0:T(8,128)(2,1)S(1)} all-reduce(f32[8,64,1024]{2,1,0:T(8,128)} %fusion.10), channel_id=1, replica_groups=mesh['group'=2,'chan'=8,'rec'=2] {'chan'}, use_global_device_ids=true, to_apply=%region_0.1 | all-reduce | flops 524288 | bytes 3145728 | tf_op jit(solution)/shard_map/psum | solution.py:31
  115.6 0.0 copy-start.2
  115.6 0.0 copy-start.3
  115.6 4.0 %fusion.8 = f32[16,64,1024]{2,1,0:T(8,128)S(1)} fusion(bf16[16,64,1024]{2,1,0:T(8,128)(2,1)S(1)} %broadcast_multiply_fusion, bf16[1024,512]{1,0:T(8,128)(2,1)} %get-tuple-element.9, bf16[1024,512]{1,0:T(8,128)(2,1)} %get-tuple-element.10), kind=kOutput, calls=%fused_computation.18 | convolution fusion | flops 2151677952 | bytes 8388608 | tf_op jit(solution)/shard_map/dot_general | solution.py:18
  119.7 0.0 copy-done.2
  119.7 0.0 copy-done.3
  119.7 1.2 fusion.9
  120.9 2.7 %fusion.20 = (f32[16,64,512]{2,1,0:T(8,128)}, f32[16,64,512]{2,1,0:T(8,128)}) fusion(f32[16,64,1024]{2,1,0:T(8,128)S(1)} %fusion.8), kind=kLoop, calls=%fused_computation.37 | loop fusion | bytes 8388608 | tf_op jit(solution)/shard_map/slice | solution.py:48
  123.7 0.2 fusion.12
  123.9 0.2 multiply_convert_fusion
  124.1 0.1 fusion.21
  124.2 0.8 copy.15
  124.9 0.8 copy.13
  125.7 4.8 %copy.14 = f32[16,64,512]{1,0,2:T(8,128)} copy(f32[16,64,512]{2,1,0:T(8,128)} %get-tuple-element.5) | data formatting | bytes 4194304 | tf_op jit(solution)/shard_map/slice | solution.py:48
  130.6 4.9 %copy.16 = f32[16,64,512]{1,0,2:T(8,128)} copy(f32[16,64,512]{2,1,0:T(8,128)} %get-tuple-element.6) | data formatting | bytes 4194304 | tf_op jit(solution)/shard_map/slice | solution.py:49
  135.5 0.0 copy-start.1
  135.5 5.4 %fusion.22 = f32[512,8,16]{2,1,0:T(8,128)S(1)} fusion(bf16[8,64,512]{1,0,2:T(8,128)(2,1)S(1)} %copy.13, f32[16,64,512]{1,0,2:T(8,128)} %copy.14), kind=kOutput, calls=%fused_computation.39 | convolution fusion | flops 50331648 | bytes 2883584 | tf_op jit(solution)/shard_map/crf,srf->csf/dot_general | solution.py:52
  140.9 0.0 copy-done.1
  140.9 3.4 %fusion.23 = f32[512,8,16]{2,1,0:T(8,128)S(1)} fusion(bf16[8,64,512]{1,0,2:T(8,128)(2,1)S(1)} %copy.13, f32[16,64,512]{1,0,2:T(8,128)S(1)} %copy-done.1), kind=kOutput, calls=%fused_computation.40 | convolution fusion | flops 50331648 | bytes 2883584 | tf_op jit(solution)/shard_map/crf,srf->csf/dot_general | solution.py:55
  144.3 0.0 copy-start
  144.3 3.4 %add_bitcast_fusion = f32[16,8,512]{0,1,2:T(8,128)S(1)} fusion(f32[512,8,16]{2,1,0:T(8,128)S(1)} %fusion.22, bf16[8,64,512]{1,0,2:T(8,128)(2,1)S(1)} %copy.15, f32[16,64,512]{1,0,2:T(8,128)S(1)} %copy-done.1), kind=kOutput, calls=%fused_computation.11 | convolution fusion | flops 50397184 | bytes 3145728 | tf_op jit(solution)/shard_map/crf,srf->csf/dot_general | solution.py:52
  147.7 0.0 copy-done
  147.7 4.7 %subtract_bitcast_fusion = f32[16,8,512]{0,1,2:T(8,128)} fusion(f32[512,8,16]{2,1,0:T(8,128)S(1)} %fusion.23, bf16[8,64,512]{1,0,2:T(8,128)(2,1)S(1)} %copy.15, f32[16,64,512]{1,0,2:T(8,128)S(1)} %copy-done), kind=kOutput, calls=%fused_computation.10 | convolution fusion | flops 50397184 | bytes 3145728 | tf_op jit(solution)/shard_map/crf,srf->csf/dot_general | solution.py:55
  152.4 2.3 %copy.22 = f32[16,8,512]{2,1,0:T(8,128)S(1)} copy(f32[16,8,512]{0,1,2:T(8,128)} %subtract_bitcast_fusion) | data formatting | bytes 524288 | tf_op jit(solution)/shard_map/sub | solution.py:55
  154.7 0.8 copy.21
  155.4 0.8 pad_maximum_fusion
  156.3 0.0 reduce-scatter.2.cloned.1.call-update
  156.3 6.6 %reduce-scatter.2.cloned.1.call-done = f32[16,8,512]{2,1,0:T(8,128)} async-done(((f32[16,8,1024]{2,1,0:T(8,128)}), f32[16,8,512]{2,1,0:T(8,128)}) %reduce-scatter.2.cloned.1.call-update) | async-done | bytes 262160 | tf_op jit(solution)/shard_map/reduce_scatter | solution.py:59
  162.8 1.7 broadcast_multiply_fusion.1
  (3 shorter events, 0.0 us)
Async XLA Ops:
  6.5 9.3 %copy-start.4 = (s32[16,64]{1,0:T(8,128)S(1)}, s32[16,64]{1,0:T(8,128)}, u32[]{:S(2)}) copy-start(s32[16,64]{1,0:T(8,128)} %param.4) | copy-start | bytes 12292
  6.5 156.3 %reduce-scatter.2.cloned.1.call-start = ((), (), s32[]{:S(2)}) async-start(), calls=%async_computation.1 | async-start | bytes 786432 | tf_op jit(solution)/shard_map/reduce_scatter | solution.py:59
  15.8 1.8 %copy-start.5 = (s32[8]{0:T(128)S(1)}, s32[8]{0:T(128)}, u32[]{:S(2)}) copy-start(s32[8]{0:T(128)} %param.5) | copy-start | bytes 100
  115.6 4.0 %copy-start.2 = (bf16[1024,512]{1,0:T(8,128)(2,1)S(1)}, bf16[1024,512]{1,0:T(8,128)(2,1)}, u32[]{:S(2)}) copy-start(bf16[1024,512]{1,0:T(8,128)(2,1)} %get-tuple-element.9) | copy-start | bytes 3145732
  115.6 4.0 %copy-start.3 = (bf16[1024,512]{1,0:T(8,128)(2,1)S(1)}, bf16[1024,512]{1,0:T(8,128)(2,1)}, u32[]{:S(2)}) copy-start(bf16[1024,512]{1,0:T(8,128)(2,1)} %get-tuple-element.10) | copy-start | bytes 3145732
  135.5 5.5 %copy-start.1 = (f32[16,64,512]{1,0,2:T(8,128)S(1)}, f32[16,64,512]{1,0,2:T(8,128)}, u32[]{:S(2)}) copy-start(f32[16,64,512]{1,0,2:T(8,128)} %copy.16) | copy-start | bytes 6291460
  144.3 3.4 %copy-start = (f32[16,64,512]{1,0,2:T(8,128)S(1)}, f32[16,64,512]{1,0,2:T(8,128)}, u32[]{:S(2)}) copy-start(f32[16,64,512]{1,0,2:T(8,128)} %copy.14) | copy-start | bytes 6291460
Sparse Core Ops, SparseCore 0:
  156.4 6.3 reduce-scatter.1
where the time goes:
time: 172 us; the launch traced here: 171 us
  blocking collectives  94.7 us (55%)
  matrix products  23.4 us (14%)
  local copies, waits for them, and re-layouts  17.1 us (10%)
  other arithmetic  15.9 us (9%)
  between operations  13.6 us (8%)
  waiting for transfers between devices  6.58 us (4%)
    psum x1, blocking collectives, spread(): return lax.psum(picked.astype(jnp.float32), 'chan').astype(jnp.bfloat16)  94.7 us
    another operation x1, other arithmetic  9.29 us
    slice x2, local copies, waits for them, and re-layouts, per_device(): xr = spectra[..., :bins]  7.57 us
    reduce_scatter x1, waiting for transfers between devices, per_device(): lax.psum_scatter(partial_stack, 'rec', scatter_dimension=2, tiled=True)  6.57 us
    dot_general x1, matrix products, per_device(): jnp.einsum('crf,srf->csf', xr, wr, precision=hp)  5.44 us
    dot_general x2, matrix products, transform(): jnp.dot(flat, table, preferred_element_type=jnp.float32)  5.26 us
    slice x1, local copies, waits for them, and re-layouts, per_device(): xi = spectra[..., bins:]  4.88 us
    dot_general x1, matrix products, per_device(): jnp.einsum('crf,srf->csf', xr, wi, precision=hp)  4.71 us
  transfers between devices with their start and end apart: 1, of which 1 were waited for; matrix products, arithmetic and copies ran while one was open for 0% of the time, Pallas kernels for 0%

commit v1 on v0

--- a/solution.py
+++ b/solution.py
@@ -1,8 +1,16 @@
+import functools
 import math
 import jax
 import jax.numpy as jnp
 from jax import lax
 from jax.sharding import PartitionSpec as P
+
+
+def save_modes(raw, mesh_dim):
+    return jnp.sum(jax.lax.all_gather(raw, mesh_dim), axis=0)
+
+
+feed_ends = functools.partial(save_modes, mesh_dim="chan")
 
 
 def dft_table(length, bins):
@@ -28,7 +36,7 @@
 
 
 def spread(picked):
-    return lax.psum(picked.astype(jnp.float32), "chan").astype(jnp.bfloat16)
+    return feed_ends(picked.astype(jnp.float32)).astype(jnp.bfloat16)
 
 
 def per_device(records, valid, sources):

time: 172 us -> 289 us (1.68)
  waiting for transfers between devices: 6.58 us -> 214 us
  blocking collectives: 94.7 us -> 0 us
  other arithmetic: 15.9 us -> 21.9 us
    all_gather x0 -> x1, waiting for transfers between devices: none -> 208 us  [save_modes(): return jnp.sum(jax.lax.all_gather(raw, mesh_dim), axis=0)]
    psum x1 -> x0, blocking collectives: 94.7 us -> none  [spread(): return lax.psum(picked.astype(jnp.float32), 'chan').astype(jnp.bfloat16)]
    reduce_sum x0 -> x1, other arithmetic: none -> 7.96 us  [save_modes(): return jnp.sum(jax.lax.all_gather(raw, mesh_dim), axis=0)]
  transfers between devices with their start and end apart: 1 -> 2, of which waited for: 1 -> 2; matrix products, arithmetic and copies ran while one was open for 0% -> 7% of each run, Pallas kernels for 0% -> 0%
where the time goes in v1:
time: 289 us
  waiting for transfers between devices  214 us (74%)
  matrix products  23.3 us (8%)
  other arithmetic  21.9 us (8%)
  local copies, waits for them, and re-layouts  16.3 us (6%)
  between operations  13.6 us (5%)
    all_gather x1, waiting for transfers between devices, save_modes(): return jnp.sum(jax.lax.all_gather(raw, mesh_dim), axis=0)  208 us
    another operation x1, other arithmetic  8.54 us
    reduce_sum x1, other arithmetic, save_modes(): return jnp.sum(jax.lax.all_gather(raw, mesh_dim), axis=0)  7.96 us
    slice x2, local copies, waits for them, and re-layouts, per_device(): xr = spectra[..., :bins]  6.83 us
    reduce_scatter x1, waiting for transfers between devices, per_device(): lax.psum_scatter(partial_stack, 'rec', scatter_dimension=2, tiled=True)  6.26 us
  transfers between devices with their start and end apart: 2, of which 2 were waited for; matrix products, arithmetic and copies ran while one was open for 7% of the time, Pallas kernels for 0%

profile of v1, /device:TPU:0, one launch (start us, length us, event | category | flops | bytes accessed | tf_op | source)
XLA Modules:
  0.0 289.1 jit_solution(3895230482152739357)
XLA Ops:
  6.5 0.0 all-gather.3.cloned.1.call-start
  6.5 0.7 convert_element_type.25
  7.2 0.0 copy-start.4
  7.2 1.8 broadcast_multiply_fusion
  9.1 0.0 copy-done.4
  9.1 2.6 fusion.11
  11.7 0.0 all-gather.3.cloned.1.call-update
  11.7 0.0 reduce-scatter.2.cloned.1.call-start
  11.8 8.5 %negate_convert_fusion = (bf16[1024,512]{1,0:T(8,128)(2,1)S(1)}, bf16[1024,512]{1,0:T(8,128)(2,1)S(1)}) fusion(), kind=kLoop, calls=%fused_computation.13 | loop fusion | flops 8912896 | bytes 2097152 | tf_op jit(solution)/shard_map/convert.2
  20.3 0.0 copy-start.2
  20.3 1.0 copy-done.2
  21.3 2.3 fusion.14
  23.6 1.8 fusion.25
  25.4 5.1 %copy.17 = f32[16,64,512]{1,0,2:T(8,128)} copy(f32[16,64,512]{2,1,0:T(8,128)} %get-tuple-element.5) | data formatting | bytes 4194304 | tf_op jit(solution)/shard_map/slice | solution.py:56
  30.5 3.8 %copy.19 = f32[16,64,512]{1,0,2:T(8,128)} copy(f32[16,64,512]{2,1,0:T(8,128)S(1)} %get-tuple-element.6) | data formatting | bytes 4194304 | tf_op jit(solution)/shard_map/slice | solution.py:57
  34.3 0.0 copy-start.3
  34.3 207.6 %all-gather.3.cloned.1.call-done = f32[64,64,1024]{2,0,1:T(8,128)} async-done(((f32[8,64,1024]{2,0,1:T(8,128)}), f32[64,64,1024]{2,0,1:T(8,128)}) %all-gather.3.cloned.1.call-update) | async-done | bytes 16777232 | tf_op jit(solution)/shard_map/all_gather | solution.py:10
  241.9 8.0 %bitcast_reduce_fusion = bf16[8,64,1024]{2,0,1:T(8,128)(2,1)S(1)} fusion(f32[64,64,1024]{2,0,1:T(8,128)} %all-gather.3.cloned.1.call-done), kind=kLoop, calls=%fused_computation | loop fusion | flops 3670016 | bytes 17825792 | tf_op jit(solution)/shard_map/reduce_sum | solution.py:10
  249.8 0.0 copy-done.3
  249.9 1.5 fusion.15
  251.4 0.2 fusion.17
  251.6 0.2 multiply_convert_fusion
  251.8 0.1 fusion.26
  251.9 0.8 copy.18
  252.7 0.8 copy.16
  253.4 0.0 copy-start.1
  253.5 5.4 %fusion.27 = f32[512,8,16]{2,1,0:T(8,128)S(1)} fusion(bf16[8,64,512]{1,0,2:T(8,128)(2,1)S(1)} %copy.16, f32[16,64,512]{1,0,2:T(8,128)} %copy.17), kind=kOutput, calls=%fused_computation.40 | convolution fusion | flops 50331648 | bytes 2883584 | tf_op jit(solution)/shard_map/crf,srf->csf/dot_general | solution.py:60
  258.9 0.0 copy-done.1
  258.9 3.4 %fusion.28 = f32[512,8,16]{2,1,0:T(8,128)S(1)} fusion(bf16[8,64,512]{1,0,2:T(8,128)(2,1)S(1)} %copy.16, f32[16,64,512]{1,0,2:T(8,128)S(1)} %copy-done.1), kind=kOutput, calls=%fused_computation.41 | convolution fusion | flops 50331648 | bytes 2883584 | tf_op jit(solution)/shard_map/crf,srf->csf/dot_general | solution.py:63
  262.3 0.0 copy-start
  262.3 3.4 %add_bitcast_fusion = f32[16,8,512]{0,1,2:T(8,128)S(1)} fusion(f32[512,8,16]{2,1,0:T(8,128)S(1)} %fusion.27, bf16[8,64,512]{1,0,2:T(8,128)(2,1)S(1)} %copy.18, f32[16,64,512]{1,0,2:T(8,128)S(1)} %copy-done.1), kind=kOutput, calls=%fused_computation.11 | convolution fusion | flops 50397184 | bytes 3145728 | tf_op jit(solution)/shard_map/crf,srf->csf/dot_general | solution.py:60
  265.7 0.0 copy-done
  265.7 4.7 %subtract_bitcast_fusion = f32[16,8,512]{0,1,2:T(8,128)} fusion(f32[512,8,16]{2,1,0:T(8,128)S(1)} %fusion.28, bf16[8,64,512]{1,0,2:T(8,128)(2,1)S(1)} %copy.18, f32[16,64,512]{1,0,2:T(8,128)S(1)} %copy-done), kind=kOutput, calls=%fused_computation.10 | convolution fusion | flops 50397184 | bytes 3145728 | tf_op jit(solution)/shard_map/crf,srf->csf/dot_general | solution.py:63
  270.4 2.3 copy.25
  272.7 0.8 copy.24
  273.4 0.8 pad_maximum_fusion
  274.3 0.0 reduce-scatter.2.cloned.1.call-update
  274.3 6.3 %reduce-scatter.2.cloned.1.call-done = f32[16,8,512]{2,1,0:T(8,128)} async-done(((f32[16,8,1024]{2,1,0:T(8,128)}), f32[16,8,512]{2,1,0:T(8,128)}) %reduce-scatter.2.cloned.1.call-update) | async-done | bytes 262160 | tf_op jit(solution)/shard_map/reduce_scatter | solution.py:67
  280.5 1.7 broadcast_multiply_fusion.1
  (2 shorter events, 0.0 us)
Async XLA Ops:
  6.5 235.3 %all-gather.3.cloned.1.call-start = ((), (), s32[]{:S(2)}) async-start(), calls=%async_computation.2 | async-start | bytes 18874368 | tf_op jit(solution)/shard_map/all_gather | solution.py:10
  7.2 1.8 copy-start.4
  11.7 268.8 %reduce-scatter.2.cloned.1.call-start = ((), (), s32[]{:S(2)}) async-start(), calls=%async_computation.1 | async-start | bytes 786432 | tf_op jit(solution)/shard_map/reduce_scatter | solution.py:67
  20.3 1.0 copy-start.2
  34.3 215.6 %copy-start.3 = (bf16[1024,512]{1,0:T(8,128)(2,1)S(1)}, bf16[1024,512]{1,0:T(8,128)(2,1)}, u32[]{:S(2)}) copy-start(bf16[1024,512]{1,0:T(8,128)(2,1)} %copy-done.2) | copy-start | bytes 3145732
  253.4 5.5 %copy-start.1 = (f32[16,64,512]{1,0,2:T(8,128)S(1)}, f32[16,64,512]{1,0,2:T(8,128)}, u32[]{:S(2)}) copy-start(f32[16,64,512]{1,0,2:T(8,128)} %copy.19) | copy-start | bytes 6291460
  262.3 3.4 %copy-start = (f32[16,64,512]{1,0,2:T(8,128)S(1)}, f32[16,64,512]{1,0,2:T(8,128)}, u32[]{:S(2)}) copy-start(f32[16,64,512]{1,0,2:T(8,128)} %copy.17) | copy-start | bytes 6291460
Sparse Core Ops, SparseCore 0:
  11.8 229.9 all-gather.2
  274.4 6.0 reduce-scatter.1
